TPU v7x, 32 devices: a whole 2x2x4 slice. The times are simulated.
32 devices in a mesh: groups: 2 (over y), seq: 4 (over z), dp: 2 (over x), mp: 2 (over core).
Axes of the slice: x: 2, y: 2, z: 4, core: 2. Of those that a mesh axis runs over, the one named last changes fastest.
Arguments:
- queries: bfloat16 [4, 512, 2048], P(('groups', 'dp'), 'seq', 'mp'), parts along dimension 0, may hold values from -6 to 6
- keys: bfloat16 [4, 512, 2048], P(('groups', 'dp'), 'seq', 'mp'), parts along dimension 0, may hold values from -6 to 6
- values: bfloat16 [4, 512, 2048], P(('groups', 'dp'), 'seq', 'mp'), parts along dimension 0, may hold values from -6 to 6
- grad_output: bfloat16 [4, 512, 2048], P(('groups', 'dp'), 'seq', 'mp'), parts along dimension 0, may hold values from -6 to 6
- counts: int32 [4, 4, 4], P(('groups', 'dp'), 'seq'), parts along dimension 0, may hold values from 0 to 64, as said below
Outputs:
- grad_queries: bfloat16 [4, 512, 2048], P(('groups', 'dp'), 'seq', 'mp'), parts along dimension 0
- grad_keys: bfloat16 [4, 512, 2048], P(('groups', 'dp'), 'seq', 'mp'), parts along dimension 0
- grad_values: bfloat16 [4, 512, 2048], P(('groups', 'dp'), 'seq', 'mp'), parts along dimension 0
There are 2 independent parts, one for each index of `groups`. A program takes and returns all parts, laid end to end along the dimension named above; each array names one. Nothing has to cross between parts.
Inputs may be any that keep to these rules, and one draw needn't show every extreme that they name: Each shard's counts sum to 128; no entry exceeds 64, some window receives 64 points from every shard.
All inputs are finite; a program needn't handle non-finite values.
Results may differ from a plain program's by a relative error of at most 0.001.
Values may be sent and summed in bfloat16 or wider, within the bound.
A program may use at most 128 MiB of HBM per device.

v0:
```python
import math
import jax
import jax.numpy as jnp
from jax import lax
from jax.sharding import PartitionSpec as P

DH = 128
highest = lax.Precision.HIGHEST


def entering(value, axis, join, neutral, backward):
    count, mine = (lax.axis_size(axis), lax.axis_index(axis))
    pieces = lax.all_gather(value, axis)
    if backward:
        pieces = pieces[::-1]
        mine = count - 1 - mine
    total = jnp.full_like(value, 0) + jnp.asarray(neutral, value.dtype)

    def hop(position, total):
        longer = join(total, pieces[position])
        return jnp.where(position < mine, longer, total)

    return lax.fori_loop(0, count - 1, hop, total)


def add_states(earlier, later):
    return earlier + later


def per_device(queries, keys, values, grad_output, counts):
    shard_count = lax.axis_size("seq")
    local_rows = queries.shape[1]
    width = queries.shape[2]
    local_heads = width // DH
    capacity = 2 * local_rows // shard_count
    window_rows = shard_count * capacity
    factor = 1.0 / math.sqrt(DH * local_rows * shard_count)
    my_counts = counts[0, 0]
    window_ends = jnp.cumsum(my_counts)
    window_starts = window_ends - my_counts
    offsets = jnp.arange(capacity, dtype=jnp.int32)
    occupied = offsets[None, :] < my_counts[:, None]
    picked = jnp.where(occupied, window_starts[:, None] + offsets[None, :], 0).reshape(-1)
    occupied_column = occupied.reshape(-1, 1)

    def pack(source):
        taken = jnp.take(source[0], picked, axis=0)
        taken = jnp.where(occupied_column, taken, jnp.zeros_like(taken))
        return taken.reshape(shard_count, capacity, width)

    def split_heads(received):
        return received.reshape(window_rows, local_heads, DH)

    def outer_sum(left, right):
        return jnp.einsum("lha,lhb->hab", left, right, preferred_element_type=jnp.float32)

    query_recv, key_recv, value_recv, grad_recv = (
        lax.all_to_all(pack(queries), "seq", split_axis=0, concat_axis=0, tiled=True),
        lax.all_to_all(pack(keys), "seq", split_axis=0, concat_axis=0, tiled=True),
        lax.all_to_all(pack(values), "seq", split_axis=0, concat_axis=0, tiled=True),
        lax.all_to_all(pack(grad_output), "seq", split_axis=0, concat_axis=0, tiled=True),
    )
    query_recv = split_heads(query_recv)
    key_recv = split_heads(key_recv)
    value_recv = split_heads(value_recv)
    grad_recv = split_heads(grad_recv)
    key_state = outer_sum(key_recv, value_recv)
    query_state = outer_sum(query_recv, grad_recv)
    zero_state = jnp.zeros((local_heads, DH, DH), jnp.float32)
    before_kv = entering(key_state, "seq", add_states, zero_state, False)
    after_qd = entering(query_state, "seq", add_states, zero_state, True)
    block = min(512, window_rows)
    nblocks = window_rows // block

    def blocked(received):
        return received.reshape(nblocks, block, local_heads, DH)

    query_blocks = blocked(query_recv)
    key_blocks = blocked(key_recv)
    value_blocks = blocked(value_recv)
    grad_blocks = blocked(grad_recv)
    block_kv = jnp.einsum(
        "nlha,nlhb->nhab", key_blocks, value_blocks, preferred_element_type=jnp.float32
    )
    block_qd = jnp.einsum(
        "nlha,nlhb->nhab", query_blocks, grad_blocks, preferred_element_type=jnp.float32
    )
    kv_before = before_kv[None] + jnp.cumsum(block_kv, axis=0) - block_kv
    qd_after = after_qd[None] + jnp.sum(block_qd, axis=0)[None] - jnp.cumsum(block_qd, axis=0)
    lower = (
        lax.broadcasted_iota(jnp.int32, (block, block), 0)
        >= lax.broadcasted_iota(jnp.int32, (block, block), 1)
    ).astype(jnp.float32)

    def one_block(pieces):
        query_part, key_part, value_part, grad_part, kv_state, qd_state = pieces
        weights = (
            jnp.einsum("rha,sha->hrs", grad_part, value_part, preferred_element_type=jnp.float32)
            * lower[None]
        )
        scores = (
            jnp.einsum("rha,sha->hrs", query_part, key_part, preferred_element_type=jnp.float32)
            * lower[None]
        )
        query_f = query_part.astype(jnp.float32)
        key_f = key_part.astype(jnp.float32)
        value_f = value_part.astype(jnp.float32)
        grad_f = grad_part.astype(jnp.float32)
        grad_q = jnp.einsum("rhb,hab->rha", grad_f, kv_state, precision=highest) + jnp.einsum(
            "hrs,sha->rha", weights, key_f, precision=highest
        )
        grad_k = jnp.einsum("shb,hab->sha", value_f, qd_state, precision=highest) + jnp.einsum(
            "hrs,rha->sha", weights, query_f, precision=highest
        )
        grad_v = jnp.einsum("sha,hab->shb", key_f, qd_state, precision=highest) + jnp.einsum(
            "hrs,rhb->shb", scores, grad_f, precision=highest
        )

        def finish(result):
            return (result * factor).astype(jnp.bfloat16).reshape(block, width)

        return (finish(grad_q), finish(grad_k), finish(grad_v))

    out_q, out_k, out_v = lax.map(
        one_block, (query_blocks, key_blocks, value_blocks, grad_blocks, kv_before, qd_after)
    )

    def to_slots(result):
        return result.reshape(shard_count, capacity, width)

    back_q, back_k, back_v = (
        lax.all_to_all(to_slots(out_q), "seq", split_axis=0, concat_axis=0, tiled=True),
        lax.all_to_all(to_slots(out_k), "seq", split_axis=0, concat_axis=0, tiled=True),
        lax.all_to_all(to_slots(out_v), "seq", split_axis=0, concat_axis=0, tiled=True),
    )
    positions = jnp.arange(local_rows, dtype=jnp.int32)
    member = (
        (positions[:, None] >= window_starts[None, :]) & (positions[:, None] < window_ends[None, :])
    ).astype(jnp.int32)
    window_of = jnp.sum(member * jnp.arange(shard_count, dtype=jnp.int32)[None, :], axis=1)
    start_of = jnp.sum(member * window_starts[None, :], axis=1)
    source_index = window_of * capacity + positions - start_of

    def unpack(returned):
        return jnp.take(returned.reshape(window_rows, width), source_index, axis=0)[None]

    return (unpack(back_q), unpack(back_k), unpack(back_v))


def solution(mesh):
    placed = (
        P(("groups", "dp"), "seq", "mp"),
        P(("groups", "dp"), "seq", "mp"),
        P(("groups", "dp"), "seq", "mp"),
        P(("groups", "dp"), "seq", "mp"),
        P(("groups", "dp"), "seq", None),
    )
    return jax.shard_map(
        per_device,
        mesh=mesh,
        in_specs=placed,
        out_specs=(
            P(("groups", "dp"), "seq", "mp"),
            P(("groups", "dp"), "seq", "mp"),
            P(("groups", "dp"), "seq", "mp"),
        ),
        check_vma=False,
    )
```

profile of v0, /device:TPU:0, one launch (start us, length us, event | category | flops | bytes accessed | tf_op | source)
XLA Modules:
  0.0 218.9 jit_solution(3963657289021872831)
XLA Ops:
  7.2 0.8 iota_compare_fusion.3
  8.0 0.8 reduce-window.7
  8.9 0.7 bitcast_subtract_fusion
  9.7 1.2 gather_fusion.4
  10.9 1.2 gather_fusion.1
  12.1 1.2 gather_fusion.2
  13.3 1.2 gather_fusion
  14.5 1.3 select_select_fusion
  15.8 20.6 %all_to_all.35 = bf16[4,64,1024]{2,1,0:T(8,128)(2,1)S(1)} all-to-all(bf16[4,64,1024]{2,1,0:T(8,128)(2,1)S(1)} %bitcast.68), channel_id=1, replica_groups=mesh['groups'=2,'seq'=4,'dp'=2,'mp'=2] {'seq'}, dimensions={0} | all-to-all | bytes 1048576 | tf_op jit(solution)/shard_map/all_to_all | solution.py:61
  36.4 3.5 %all-to-all-start.4 = ((bf16[4,64,1024]{2,1,0:T(8,128)(2,1)}), bf16[4,64,1024]{2,1,0:T(8,128)(2,1)S(1)}, u32[]{:S(2)}, u32[]{:S(2)}) async-start(bf16[4,64,1024]{2,1,0:T(8,128)(2,1)} %bitcast.14), calls=%async_computation.4 | async-start | bytes 1048576 | tf_op jit(solution)/shard_map/all_to_all | solution.py:58
  40.4 13.1 %all-to-all-done.4 = bf16[4,64,1024]{2,1,0:T(8,128)(2,1)S(1)} async-done(((bf16[4,64,1024]{2,1,0:T(8,128)(2,1)}), bf16[4,64,1024]{2,1,0:T(8,128)(2,1)S(1)}, u32[]{:S(2)}, u32[]{:S(2)}) %all-to-all-start.4) | async-done | bytes 524320 | tf_op jit(solution)/shard_map/all_to_all | solution.py:58
  53.6 1.2 fusion.47
  54.8 27.9 %all_to_all.36 = bf16[4,64,1024]{2,1,0:T(8,128)(2,1)S(1)} all-to-all(bf16[4,64,1024]{2,1,0:T(8,128)(2,1)S(1)} %bitcast.67), channel_id=1, replica_groups=mesh['groups'=2,'seq'=4,'dp'=2,'mp'=2] {'seq'}, dimensions={0} | all-to-all | bytes 1048576 | tf_op jit(solution)/shard_map/all_to_all | solution.py:59
  82.7 4.1 %all-to-all-start.1 = ((bf16[4,64,1024]{2,1,0:T(8,128)(2,1)}), bf16[4,64,1024]{2,1,0:T(8,128)(2,1)S(1)}, u32[]{:S(2)}, u32[]{:S(2)}) async-start(bf16[4,64,1024]{2,1,0:T(8,128)(2,1)} %bitcast.6), calls=%async_computation.1 | async-start | bytes 1048576 | tf_op jit(solution)/shard_map/all_to_all | solution.py:60
  87.0 25.5 %all-to-all-done.1 = bf16[4,64,1024]{2,1,0:T(8,128)(2,1)S(1)} async-done(((bf16[4,64,1024]{2,1,0:T(8,128)(2,1)}), bf16[4,64,1024]{2,1,0:T(8,128)(2,1)S(1)}, u32[]{:S(2)}, u32[]{:S(2)}) %all-to-all-start.1) | async-done | bytes 524320 | tf_op jit(solution)/shard_map/all_to_all | solution.py:60
  112.4 0.9 copy.70
  113.3 2.2 fusion.55
  115.6 1.8 fusion.49
  117.4 3.2 %rev.3 = f32[4,8,128,128]{3,2,1,0:T(8,128)} reverse(f32[4,8,128,128]{3,2,1,0:T(8,128)} %bitcast.69), dimensions={0} | reverse | bytes 4194304 | tf_op jit(solution)/shard_map/rev | solution.py:15
  120.7 3.8 %while.35 = (s32[]{:T(128)}, f32[8,128,128]{2,1,0:T(8,128)S(1)}, s32[]{:T(128)}, f32[4,8,128,128]{3,2,1,0:T(8,128)}, s32[]{:T(128)}, /*index=5*/s32[]{:T(128)}) while((s32[]{:T(128)}, f32[8,128,128]{2,1,0:T(8,128)S(1)}, s32[]{:T(128)}, f32[4,8,128,128]{3,2,1,0:T(8,128)}, s32[]{:T(128)}, /*index=5*/s32[]{:T(128)}) %tuple.75), condition=%wide.region_6.9_spmd.clone, body=%wide.region_5.8_spmd.clone.sunk | while | flops 393220 | bytes 1572965 | solution.py:23
  120.7 1.3 add_select_fusion.5
  122.0 1.2 add_select_fusion.5
  123.2 1.3 add_select_fusion.5
  125.2 1.0 copy-done.12
  126.1 1.1 fusion.39
  127.5 1.0 reshape.172
  128.6 4.1 %all-to-all-start.6 = ((bf16[4,64,1024]{2,1,0:T(8,128)(2,1)}), bf16[4,64,1024]{2,1,0:T(8,128)(2,1)}, u32[]{:S(2)}, u32[]{:S(2)}) async-start(bf16[4,64,1024]{2,1,0:T(8,128)(2,1)} %reshape.172), calls=%async_computation.6 | async-start | bytes 1048576 | tf_op jit(solution)/shard_map/all_to_all | solution.py:134
  132.7 1.8 fusion.53
  134.5 1.7 fusion.51
  136.2 1.2 fusion.36
  137.4 1.1 copy.61
  138.5 2.1 reshape.170
  140.6 21.8 %all-to-all-done.6 = bf16[4,64,1024]{2,1,0:T(8,128)(2,1)} async-done(((bf16[4,64,1024]{2,1,0:T(8,128)(2,1)}), bf16[4,64,1024]{2,1,0:T(8,128)(2,1)}, u32[]{:S(2)}, u32[]{:S(2)}) %all-to-all-start.6) | async-done | bytes 524320 | tf_op jit(solution)/shard_map/all_to_all | solution.py:134
  162.4 4.3 %all-to-all-start.5 = ((bf16[4,64,1024]{2,1,0:T(8,128)(2,1)}), bf16[4,64,1024]{2,1,0:T(8,128)(2,1)}, u32[]{:S(2)}, u32[]{:S(2)}) async-start(bf16[4,64,1024]{2,1,0:T(8,128)(2,1)} %reshape.170), calls=%async_computation.5 | async-start | bytes 1048576 | tf_op jit(solution)/shard_map/all_to_all | solution.py:133
  166.7 17.4 %all-gather.5.cloned.1.call-done = f32[32,128,128]{2,1,0:T(8,128)} async-done(((f32[8,128,128]{2,1,0:T(8,128)}), f32[32,128,128]{2,1,0:T(8,128)}) %all-gather.5.cloned.1.call-update) | async-done | bytes 2097168 | tf_op jit(solution)/shard_map/all_gather | solution.py:13
  184.1 3.8 %while.34 = (s32[]{:T(128)}, f32[8,128,128]{2,1,0:T(8,128)S(1)}, s32[]{:T(128)}, f32[4,8,128,128]{3,2,1,0:T(8,128)}, s32[]{:T(128)}, /*index=5*/s32[]{:T(128)}) while((s32[]{:T(128)}, f32[8,128,128]{2,1,0:T(8,128)S(1)}, s32[]{:T(128)}, f32[4,8,128,128]{3,2,1,0:T(8,128)}, s32[]{:T(128)}, /*index=5*/s32[]{:T(128)}) %tuple.85), condition=%wide.region_2.4_spmd.clone, body=%wide.region_1.3_spmd.clone.sunk | while | flops 393220 | bytes 1572965 | solution.py:23
  184.1 1.3 add_select_fusion.4
  185.4 1.2 add_select_fusion.4
  186.7 1.2 add_select_fusion.4
  187.9 1.7 fusion.45
  189.6 1.4 fusion.33
  191.4 1.0 reshape.166
  192.5 3.5 %all-to-all-start.3 = ((bf16[4,64,1024]{2,1,0:T(8,128)(2,1)}), bf16[4,64,1024]{2,1,0:T(8,128)(2,1)S(1)}, u32[]{:S(2)}, u32[]{:S(2)}) async-start(bf16[4,64,1024]{2,1,0:T(8,128)(2,1)} %reshape.166), calls=%async_computation.3 | async-start | bytes 1048576 | tf_op jit(solution)/shard_map/all_to_all | solution.py:132
  196.0 2.2 gather_fusion.6
  198.2 2.2 gather_fusion.5
  200.4 9.9 %all-to-all-done.3 = bf16[4,64,1024]{2,1,0:T(8,128)(2,1)S(1)} async-done(((bf16[4,64,1024]{2,1,0:T(8,128)(2,1)}), bf16[4,64,1024]{2,1,0:T(8,128)(2,1)S(1)}, u32[]{:S(2)}, u32[]{:S(2)}) %all-to-all-start.3) | async-done | bytes 524320 | tf_op jit(solution)/shard_map/all_to_all | solution.py:132
  210.2 0.9 gather_fusion.3
  211.1 1.0 select_bitcast_fusion
  (55 shorter events, 2.4 us)
Async XLA Ops:
  7.2 2.5 %copy-start = (bf16[1,128,1024]{2,1,0:T(8,128)(2,1)S(1)}, bf16[1,128,1024]{2,1,0:T(8,128)(2,1)}, u32[]{:S(2)}) copy-start(bf16[1,128,1024]{2,1,0:T(8,128)(2,1)} %param.13) | copy-start | bytes 786436
  9.7 1.2 copy-start.1
  10.9 1.2 copy-start.2
  12.1 1.2 copy-start.3
  36.4 17.1 %all-to-all-start.4 = ((bf16[4,64,1024]{2,1,0:T(8,128)(2,1)}), bf16[4,64,1024]{2,1,0:T(8,128)(2,1)S(1)}, u32[]{:S(2)}, u32[]{:S(2)}) async-start(bf16[4,64,1024]{2,1,0:T(8,128)(2,1)} %bitcast.14), calls=%async_computation.4 | async-start | bytes 1048576 | tf_op jit(solution)/shard_map/all_to_all | solution.py:58
  39.9 77.6 %all-gather.7.cloned.1.call-start = ((), (), s32[]{:S(2)}) async-start(), calls=%async_computation.8 | async-start | bytes 2621440 | tf_op jit(solution)/shard_map/all_gather | solution.py:13
  40.3 84.8 %copy-start.4 = (bf16[256,8,128]{0,2,1:T(8,128)(2,1)}, bf16[256,8,128]{0,2,1:T(8,128)(2,1)S(1)}, u32[]{:S(2)}) copy-start(bf16[256,8,128]{0,2,1:T(8,128)(2,1)S(1)} %copy.66) | copy-start | bytes 1572868
  53.6 62.0 %copy-start.10 = (bf16[32,8,8,128]{3,2,1,0:T(8,128)(2,1)}, bf16[32,8,8,128]{3,2,1,0:T(8,128)(2,1)S(1)}, u32[]{:S(2)}) copy-start(bf16[32,8,8,128]{3,2,1,0:T(8,128)(2,1)S(1)} %copy.72) | copy-start | bytes 1572868
  82.7 29.7 %all-to-all-start.1 = ((bf16[4,64,1024]{2,1,0:T(8,128)(2,1)}), bf16[4,64,1024]{2,1,0:T(8,128)(2,1)S(1)}, u32[]{:S(2)}, u32[]{:S(2)}) async-start(bf16[4,64,1024]{2,1,0:T(8,128)(2,1)} %bitcast.6), calls=%async_computation.1 | async-start | bytes 1048576 | tf_op jit(solution)/shard_map/all_to_all | solution.py:60
  86.9 97.3 %all-gather.5.cloned.1.call-start = ((), (), s32[]{:S(2)}) async-start(), calls=%async_computation.7 | async-start | bytes 2621440 | tf_op jit(solution)/shard_map/all_gather | solution.py:13
  87.0 37.5 %copy-start.6 = (bf16[32,8,8,128]{3,2,1,0:T(8,128)(2,1)}, bf16[32,8,8,128]{3,2,1,0:T(8,128)(2,1)S(1)}, u32[]{:S(2)}) copy-start(bf16[32,8,8,128]{3,2,1,0:T(8,128)(2,1)S(1)} %copy.69) | copy-start | bytes 1572868
  115.6 9.5 %copy-start.13 = (f32[256,256]{1,0:T(8,128)}, f32[256,256]{1,0:T(8,128)S(1)}, u32[]{:S(2)}) copy-start(f32[256,256]{1,0:T(8,128)S(1)} %fusion.62) | copy-start | bytes 786436
  120.7 3.9 %copy-start.8 = (f32[8,128,128]{2,1,0:T(8,128)S(1)}, f32[8,128,128]{2,1,0:T(8,128)}, u32[]{:S(2)}) copy-start(f32[8,128,128]{2,1,0:T(8,128)} %fusion.47) | copy-start | bytes 1572868
  124.5 1.7 copy-start.12
  128.6 33.8 %all-to-all-start.6 = ((bf16[4,64,1024]{2,1,0:T(8,128)(2,1)}), bf16[4,64,1024]{2,1,0:T(8,128)(2,1)}, u32[]{:S(2)}, u32[]{:S(2)}) async-start(bf16[4,64,1024]{2,1,0:T(8,128)(2,1)} %reshape.172), calls=%async_computation.6 | async-start | bytes 1048576 | tf_op jit(solution)/shard_map/all_to_all | solution.py:134
  132.7 1.8 copy-start.9
  134.5 1.7 copy-start.11
  134.5 1.7 copy-start.14
  162.4 30.1 %all-to-all-start.5 = ((bf16[4,64,1024]{2,1,0:T(8,128)(2,1)}), bf16[4,64,1024]{2,1,0:T(8,128)(2,1)}, u32[]{:S(2)}, u32[]{:S(2)}) async-start(bf16[4,64,1024]{2,1,0:T(8,128)(2,1)} %reshape.170), calls=%async_computation.5 | async-start | bytes 1048576 | tf_op jit(solution)/shard_map/all_to_all | solution.py:133
  184.1 3.8 %copy-start.5 = (bf16[256,8,128]{0,2,1:T(8,128)(2,1)S(1)}, bf16[256,8,128]{0,2,1:T(8,128)(2,1)}, u32[]{:S(2)}) copy-start(bf16[256,8,128]{0,2,1:T(8,128)(2,1)} %copy-done.4) | copy-start | bytes 1572868
  187.9 1.7 copy-start.7
  187.9 1.7 copy-start.15
  192.5 17.8 %all-to-all-start.3 = ((bf16[4,64,1024]{2,1,0:T(8,128)(2,1)}), bf16[4,64,1024]{2,1,0:T(8,128)(2,1)S(1)}, u32[]{:S(2)}, u32[]{:S(2)}) async-start(bf16[4,64,1024]{2,1,0:T(8,128)(2,1)} %reshape.166), calls=%async_computation.3 | async-start | bytes 1048576 | tf_op jit(solution)/shard_map/all_to_all | solution.py:132
Sparse Core Ops, SparseCore 0:
  54.9 61.5 all-gather.6
  118.1 65.9 all-gather.4
where the time goes:
time: 220 us; the launch traced here: 219 us
  waiting for transfers between devices  87.7 us (40%)
  blocking collectives  48.5 us (22%)
  local copies, waits for them, and re-layouts  21.6 us (10%)
  starting transfers between devices  19.6 us (9%)
  matrix products  14.6 us (7%)
  between operations  14.5 us (7%)
  other arithmetic  12.3 us (6%)
    all_to_all x1, blocking collectives, per_device(): lax.all_to_all(pack(keys), 'seq', split_axis=0, concat_axis=0, tiled=True)  27.9 us
    all_to_all x1, waiting for transfers between devices, per_device(): lax.all_to_all(pack(values), 'seq', split_axis=0, concat_axis=0, tiled=True)  25.5 us
    all_to_all x1, waiting for transfers between devices, per_device(): lax.all_to_all(to_slots(out_v), 'seq', split_axis=0, concat_axis=0, tiled...  21.8 us
    all_to_all x1, blocking collectives, per_device(): lax.all_to_all(pack(grad_output), 'seq', split_axis=0, concat_axis=0, til...  20.6 us
    all_gather x2, waiting for transfers between devices, entering(): pieces = lax.all_gather(value, axis)  17.4 us
    all_to_all x1, waiting for transfers between devices, per_device(): lax.all_to_all(pack(queries), 'seq', split_axis=0, concat_axis=0, tiled=T...  13.1 us
    all_to_all x1, waiting for transfers between devices, per_device(): lax.all_to_all(to_slots(out_q), 'seq', split_axis=0, concat_axis=0, tiled...  9.87 us
    select_n x6, other arithmetic, hop(): return jnp.where(position < mine, longer, total)  7.5 us
  transfers between devices with their start and end apart: 7, of which 5 were waited for; matrix products, arithmetic and copies ran while one was open for 16% of the time, Pallas kernels for 0%

commit v1 on v0

--- a/solution.py
+++ b/solution.py
@@ -1,3 +1,4 @@
+import functools
 import math
 import jax
 import jax.numpy as jnp
@@ -6,6 +7,29 @@
 
 DH = 128
 highest = lax.Precision.HIGHEST
+
+
+def rest_things_all(x0, row_dim, axis_k):
+    latest = jax.lax.axis_index("seq")
+    y2 = jax.lax.axis_size("seq")
+    z, tall = (y2, latest)
+    b_next = x0.shape[row_dim] // z
+    upper = list(x0.shape)
+    upper[row_dim] = b_next
+    vec_out = upper[axis_k]
+    upper[axis_k] = vec_out * z
+    current_arr = jnp.zeros(upper, x0.dtype)
+    for num in range(z):
+        frame_out = lax.dynamic_slice_in_dim(x0, (tall ^ num) * b_next, b_next, axis=row_dim)
+        if num:
+            frame_out = jax.lax.ppermute(frame_out, "seq", [(t, t ^ num) for t in range(z)])
+        current_arr = lax.dynamic_update_slice_in_dim(
+            current_arr, frame_out, (tall ^ num) * vec_out, axis=axis_k
+        )
+    return current_arr
+
+
+prepare_corner_on = functools.partial(rest_things_all, row_dim=0, axis_k=0)
 
 
 def entering(value, axis, join, neutral, backward):
@@ -57,7 +81,7 @@
     query_recv, key_recv, value_recv, grad_recv = (
         lax.all_to_all(pack(queries), "seq", split_axis=0, concat_axis=0, tiled=True),
         lax.all_to_all(pack(keys), "seq", split_axis=0, concat_axis=0, tiled=True),
-        lax.all_to_all(pack(values), "seq", split_axis=0, concat_axis=0, tiled=True),
+        prepare_corner_on(pack(values)),
         lax.all_to_all(pack(grad_output), "seq", split_axis=0, concat_axis=0, tiled=True),
     )
     query_recv = split_heads(query_recv)

time: 220 us -> 221 us (level)
  blocking collectives: 48.5 us -> 20.6 us
  waiting for transfers between devices: 87.7 us -> 115 us
  starting transfers between devices: 19.6 us -> 23.4 us
    ppermute x0 -> x3, waiting for transfers between devices: none -> 35.6 us  [rest_things_all(): jax.lax.ppermute(frame_out, 'seq', [(t, t ^ num) for t in range(z)])]
    all_to_all x1 -> x0, blocking collectives: 27.9 us -> none  [per_device(): lax.all_to_all(pack(keys), 'seq', split_axis=0, concat_axis=0, tiled=True)]
    all_to_all x1, waiting for transfers between devices: 25.5 us -> 0.01 us  [per_device(): lax.all_to_all(pack(keys), 'seq', split_axis=0, concat_axis=0, tiled=True)]
    all_gather x2, waiting for transfers between devices: 17.4 us -> 34.5 us  [entering(): pieces = lax.all_gather(value, axis)]
    ppermute x0 -> x3, starting transfers between devices: none -> 4.45 us  [rest_things_all(): jax.lax.ppermute(frame_out, 'seq', [(t, t ^ num) for t in range(z)])]
  transfers between devices with their start and end apart: 7 -> 10, of which waited for: 5 -> 7; matrix products, arithmetic and copies ran while one was open for 16% -> 15% of each run, Pallas kernels for 0% -> 0%
where the time goes in v1:
time: 221 us; the launch traced here: 220 us
  waiting for transfers between devices  115 us (52%)
  starting transfers between devices  23.4 us (11%)
  local copies, waits for them, and re-layouts  21.5 us (10%)
  blocking collectives  20.6 us (9%)
  between operations  14.6 us (7%)
  matrix products  12.5 us (6%)
  other arithmetic  12.3 us (6%)
    ppermute x3, waiting for transfers between devices, rest_things_all(): jax.lax.ppermute(frame_out, 'seq', [(t, t ^ num) for t in range(z)])  35.6 us
    all_gather x2, waiting for transfers between devices, entering(): pieces = lax.all_gather(value, axis)  34.5 us
    all_to_all x1, waiting for transfers between devices, per_device(): lax.all_to_all(to_slots(out_v), 'seq', split_axis=0, concat_axis=0, tiled...  21.7 us
    all_to_all x1, blocking collectives, per_device(): lax.all_to_all(pack(grad_output), 'seq', split_axis=0, concat_axis=0, til...  20.6 us
    all_to_all x1, waiting for transfers between devices, per_device(): lax.all_to_all(pack(queries), 'seq', split_axis=0, concat_axis=0, tiled=T...  13.1 us
    all_to_all x1, waiting for transfers between devices, per_device(): lax.all_to_all(to_slots(out_q), 'seq', split_axis=0, concat_axis=0, tiled...  9.86 us
    select_n x6, other arithmetic, hop(): return jnp.where(position < mine, longer, total)  7.47 us
    gather x3, local copies, waits for them, and re-layouts, unpack(): jnp.take(returned.reshape(window_rows, width), source_index, axis=0)[None]  5.17 us
  transfers between devices with their start and end apart: 10, of which 7 were waited for; matrix products, arithmetic and copies ran while one was open for 15% of the time, Pallas kernels for 0%

profile of v1, /device:TPU:0, one launch (start us, length us, event | category | flops | bytes accessed | tf_op | source)
XLA Modules:
  0.0 219.7 jit_solution(9074986719932527272)
XLA Ops:
  7.2 0.8 iota_compare_fusion.3
  8.0 0.8 reduce-window.7
  9.7 1.2 gather_fusion.4
  10.9 1.2 gather_fusion.1
  12.1 1.2 gather_fusion.2
  13.3 1.2 gather_fusion
  14.5 1.3 select_select_fusion
  15.8 20.6 %all_to_all.30 = bf16[4,64,1024]{2,1,0:T(8,128)(2,1)S(1)} all-to-all(bf16[4,64,1024]{2,1,0:T(8,128)(2,1)S(1)} %bitcast.71), channel_id=1, replica_groups=mesh['groups'=2,'seq'=4,'dp'=2,'mp'=2] {'seq'}, dimensions={0} | all-to-all | bytes 1048576 | tf_op jit(solution)/shard_map/all_to_all | solution.py:85
  36.4 3.5 %all-to-all-start.3 = ((bf16[4,64,1024]{2,1,0:T(8,128)(2,1)}), bf16[4,64,1024]{2,1,0:T(8,128)(2,1)S(1)}, u32[]{:S(2)}, u32[]{:S(2)}) async-start(bf16[4,64,1024]{2,1,0:T(8,128)(2,1)} %bitcast.14), calls=%async_computation.3 | async-start | bytes 1048576 | tf_op jit(solution)/shard_map/all_to_all | solution.py:82
  40.3 13.1 %all-to-all-done.3 = bf16[4,64,1024]{2,1,0:T(8,128)(2,1)S(1)} async-done(((bf16[4,64,1024]{2,1,0:T(8,128)(2,1)}), bf16[4,64,1024]{2,1,0:T(8,128)(2,1)S(1)}, u32[]{:S(2)}, u32[]{:S(2)}) %all-to-all-start.3) | async-done | bytes 524320 | tf_op jit(solution)/shard_map/all_to_all | solution.py:82
  53.6 1.2 fusion.47
  54.7 3.5 %all-to-all-start = ((bf16[4,64,1024]{2,1,0:T(8,128)(2,1)}), bf16[4,64,1024]{2,1,0:T(8,128)(2,1)S(1)}, u32[]{:S(2)}, u32[]{:S(2)}) async-start(bf16[4,64,1024]{2,1,0:T(8,128)(2,1)} %bitcast.4), calls=%async_computation | async-start | bytes 1048576 | tf_op jit(solution)/shard_map/all_to_all | solution.py:83
  58.4 2.0 collective-permute-start
  60.4 2.4 %collective-permute-start.1 = (bf16[1,64,1024]{2,1,0:T(8,128)(2,1)S(1)}, bf16[1,64,1024]{2,1,0:T(8,128)(2,1)S(1)}, u32[]{:S(2)}, u32[]{:S(2)}) collective-permute-start(bf16[1,64,1024]{2,1,0:T(8,128)(2,1)S(1)} %get-tuple-element.251), channel_id=1, source_target_pairs={{0,8},{4,12},{8,0},{12,4},{1,9},{5,13},{9,1},{13,5},{2,10},{6,14},... | collective-permute-start | bytes 393224 | tf_op jit(solution)/shard_map/ppermute | solution.py:25
  62.9 16.4 %collective-permute-done = bf16[1,64,1024]{2,1,0:T(8,128)(2,1)S(1)} collective-permute-done((bf16[1,64,1024]{2,1,0:T(8,128)(2,1)S(1)}, bf16[1,64,1024]{2,1,0:T(8,128)(2,1)S(1)}, u32[]{:S(2)}, u32[]{:S(2)}) %collective-permute-start) | collective-permute-done | bytes 131104 | tf_op jit(solution)/shard_map/ppermute | solution.py:25
  79.3 19.2 %collective-permute-done.1 = bf16[1,64,1024]{2,1,0:T(8,128)(2,1)S(1)} collective-permute-done((bf16[1,64,1024]{2,1,0:T(8,128)(2,1)S(1)}, bf16[1,64,1024]{2,1,0:T(8,128)(2,1)S(1)}, u32[]{:S(2)}, u32[]{:S(2)}) %collective-permute-start.1) | collective-permute-done | bytes 131104 | tf_op jit(solution)/shard_map/ppermute | solution.py:25
  98.7 1.1 fusion.55
  100.0 1.8 fusion.49
  101.8 15.7 %all-gather.7.cloned.1.call-done = f32[32,128,128]{2,1,0:T(8,128)} async-done(((f32[8,128,128]{2,1,0:T(8,128)}), f32[32,128,128]{2,1,0:T(8,128)}) %all-gather.7.cloned.1.call-update) | async-done | bytes 2097168 | tf_op jit(solution)/shard_map/all_gather | solution.py:37
  117.5 3.2 %rev.3 = f32[4,8,128,128]{3,2,1,0:T(8,128)} reverse(f32[4,8,128,128]{3,2,1,0:T(8,128)} %bitcast.72), dimensions={0} | reverse | bytes 4194304 | tf_op jit(solution)/shard_map/rev | solution.py:39
  120.7 3.8 %while.35 = (s32[]{:T(128)}, f32[8,128,128]{2,1,0:T(8,128)S(1)}, s32[]{:T(128)}, f32[4,8,128,128]{3,2,1,0:T(8,128)}, s32[]{:T(128)}, /*index=5*/s32[]{:T(128)}) while((s32[]{:T(128)}, f32[8,128,128]{2,1,0:T(8,128)S(1)}, s32[]{:T(128)}, f32[4,8,128,128]{3,2,1,0:T(8,128)}, s32[]{:T(128)}, /*index=5*/s32[]{:T(128)}) %tuple.78), condition=%wide.region_6.9_spmd.clone, body=%wide.region_5.8_spmd.clone.sunk | while | flops 393220 | bytes 1572965 | solution.py:47
  120.7 1.3 add_select_fusion.5
  122.0 1.2 add_select_fusion.5
  123.3 1.2 add_select_fusion.5
  125.2 1.1 copy-done.14
  126.3 1.1 fusion.39
  127.6 1.0 reshape.172
  128.7 4.1 %all-to-all-start.5 = ((bf16[4,64,1024]{2,1,0:T(8,128)(2,1)}), bf16[4,64,1024]{2,1,0:T(8,128)(2,1)}, u32[]{:S(2)}, u32[]{:S(2)}) async-start(bf16[4,64,1024]{2,1,0:T(8,128)(2,1)} %reshape.172), calls=%async_computation.5 | async-start | bytes 1048576 | tf_op jit(solution)/shard_map/all_to_all | solution.py:158
  132.8 1.8 fusion.53
  135.7 1.2 fusion.36
  136.9 1.1 copy.61
  138.0 2.0 reshape.170
  140.1 21.7 %all-to-all-done.5 = bf16[4,64,1024]{2,1,0:T(8,128)(2,1)} async-done(((bf16[4,64,1024]{2,1,0:T(8,128)(2,1)}), bf16[4,64,1024]{2,1,0:T(8,128)(2,1)}, u32[]{:S(2)}, u32[]{:S(2)}) %all-to-all-start.5) | async-done | bytes 524320 | tf_op jit(solution)/shard_map/all_to_all | solution.py:158
  161.8 4.3 %all-to-all-start.4 = ((bf16[4,64,1024]{2,1,0:T(8,128)(2,1)}), bf16[4,64,1024]{2,1,0:T(8,128)(2,1)}, u32[]{:S(2)}, u32[]{:S(2)}) async-start(bf16[4,64,1024]{2,1,0:T(8,128)(2,1)} %reshape.170), calls=%async_computation.4 | async-start | bytes 1048576 | tf_op jit(solution)/shard_map/all_to_all | solution.py:157
  166.1 18.8 %all-gather.5.cloned.1.call-done = f32[32,128,128]{2,1,0:T(8,128)} async-done(((f32[8,128,128]{2,1,0:T(8,128)}), f32[32,128,128]{2,1,0:T(8,128)}) %all-gather.5.cloned.1.call-update) | async-done | bytes 2097168 | tf_op jit(solution)/shard_map/all_gather | solution.py:37
  184.9 3.8 %while.34 = (s32[]{:T(128)}, f32[8,128,128]{2,1,0:T(8,128)S(1)}, s32[]{:T(128)}, f32[4,8,128,128]{3,2,1,0:T(8,128)}, s32[]{:T(128)}, /*index=5*/s32[]{:T(128)}) while((s32[]{:T(128)}, f32[8,128,128]{2,1,0:T(8,128)S(1)}, s32[]{:T(128)}, f32[4,8,128,128]{3,2,1,0:T(8,128)}, s32[]{:T(128)}, /*index=5*/s32[]{:T(128)}) %tuple.88), condition=%wide.region_2.4_spmd.clone, body=%wide.region_1.3_spmd.clone.sunk | while | flops 393220 | bytes 1572965 | solution.py:47
  184.9 1.3 add_select_fusion.4
  186.2 1.2 add_select_fusion.4
  187.4 1.2 add_select_fusion.4
  188.7 1.7 fusion.45
  190.4 1.4 fusion.33
  192.2 1.0 reshape.166
  193.2 3.5 %all-to-all-start.2 = ((bf16[4,64,1024]{2,1,0:T(8,128)(2,1)}), bf16[4,64,1024]{2,1,0:T(8,128)(2,1)S(1)}, u32[]{:S(2)}, u32[]{:S(2)}) async-start(bf16[4,64,1024]{2,1,0:T(8,128)(2,1)} %reshape.166), calls=%async_computation.2 | async-start | bytes 1048576 | tf_op jit(solution)/shard_map/all_to_all | solution.py:156
  196.8 2.2 gather_fusion.6
  199.0 2.2 gather_fusion.5
  201.1 9.9 %all-to-all-done.2 = bf16[4,64,1024]{2,1,0:T(8,128)(2,1)S(1)} async-done(((bf16[4,64,1024]{2,1,0:T(8,128)(2,1)}), bf16[4,64,1024]{2,1,0:T(8,128)(2,1)S(1)}, u32[]{:S(2)}, u32[]{:S(2)}) %all-to-all-start.2) | async-done | bytes 524320 | tf_op jit(solution)/shard_map/all_to_all | solution.py:156
  211.0 0.9 gather_fusion.3
  211.8 1.0 select_bitcast_fusion
  (69 shorter events, 4.5 us)
Async XLA Ops:
  7.2 2.5 %copy-start = (bf16[1,128,1024]{2,1,0:T(8,128)(2,1)S(1)}, bf16[1,128,1024]{2,1,0:T(8,128)(2,1)}, u32[]{:S(2)}) copy-start(bf16[1,128,1024]{2,1,0:T(8,128)(2,1)} %param.13) | copy-start | bytes 786436
  9.7 1.2 copy-start.1
  10.9 1.2 copy-start.2
  12.1 1.2 copy-start.3
  36.4 17.1 %all-to-all-start.3 = ((bf16[4,64,1024]{2,1,0:T(8,128)(2,1)}), bf16[4,64,1024]{2,1,0:T(8,128)(2,1)S(1)}, u32[]{:S(2)}, u32[]{:S(2)}) async-start(bf16[4,64,1024]{2,1,0:T(8,128)(2,1)} %bitcast.14), calls=%async_computation.3 | async-start | bytes 1048576 | tf_op jit(solution)/shard_map/all_to_all | solution.py:82
  39.9 77.6 %all-gather.7.cloned.1.call-start = ((), (), s32[]{:S(2)}) async-start(), calls=%async_computation.7 | async-start | bytes 2621440 | tf_op jit(solution)/shard_map/all_gather | solution.py:37
  40.3 84.8 %copy-start.4 = (bf16[256,8,128]{0,2,1:T(8,128)(2,1)}, bf16[256,8,128]{0,2,1:T(8,128)(2,1)S(1)}, u32[]{:S(2)}) copy-start(bf16[256,8,128]{0,2,1:T(8,128)(2,1)S(1)} %copy.66) | copy-start | bytes 1572868
  53.6 46.4 %copy-start.10 = (bf16[32,8,8,128]{3,2,1,0:T(8,128)(2,1)}, bf16[32,8,8,128]{3,2,1,0:T(8,128)(2,1)S(1)}, u32[]{:S(2)}) copy-start(bf16[32,8,8,128]{3,2,1,0:T(8,128)(2,1)S(1)} %copy.72) | copy-start | bytes 1572868
  54.7 43.9 %all-to-all-start = ((bf16[4,64,1024]{2,1,0:T(8,128)(2,1)}), bf16[4,64,1024]{2,1,0:T(8,128)(2,1)S(1)}, u32[]{:S(2)}, u32[]{:S(2)}) async-start(bf16[4,64,1024]{2,1,0:T(8,128)(2,1)} %bitcast.4), calls=%async_computation | async-start | bytes 1048576 | tf_op jit(solution)/shard_map/all_to_all | solution.py:83
  58.2 126.6 %all-gather.5.cloned.1.call-start = ((), (), s32[]{:S(2)}) async-start(), calls=%async_computation.6 | async-start | bytes 2621440 | tf_op jit(solution)/shard_map/all_gather | solution.py:37
  58.4 20.8 %collective-permute-start = (bf16[1,64,1024]{2,1,0:T(8,128)(2,1)S(1)}, bf16[1,64,1024]{2,1,0:T(8,128)(2,1)S(1)}, u32[]{:S(2)}, u32[]{:S(2)}) collective-permute-start(bf16[1,64,1024]{2,1,0:T(8,128)(2,1)S(1)} %get-tuple-element.252), channel_id=1, source_target_pairs={{0,4},{4,0},{8,12},{12,8},{1,5},{5,1},{9,13},{13,9},{2,6},{6,2},{1... | collective-permute-start | bytes 393224 | tf_op jit(solution)/shard_map/ppermute | solution.py:25
  60.4 38.0 %collective-permute-start.1 = (bf16[1,64,1024]{2,1,0:T(8,128)(2,1)S(1)}, bf16[1,64,1024]{2,1,0:T(8,128)(2,1)S(1)}, u32[]{:S(2)}, u32[]{:S(2)}) collective-permute-start(bf16[1,64,1024]{2,1,0:T(8,128)(2,1)S(1)} %get-tuple-element.251), channel_id=1, source_target_pairs={{0,8},{4,12},{8,0},{12,4},{1,9},{5,13},{9,1},{13,5},{2,10},{6,14},... | collective-permute-start | bytes 393224 | tf_op jit(solution)/shard_map/ppermute | solution.py:25
  62.8 35.7 %collective-permute-start.2 = (bf16[1,64,1024]{2,1,0:T(8,128)(2,1)S(1)}, bf16[1,64,1024]{2,1,0:T(8,128)(2,1)S(1)}, u32[]{:S(2)}, u32[]{:S(2)}) collective-permute-start(bf16[1,64,1024]{2,1,0:T(8,128)(2,1)S(1)} %get-tuple-element.250), channel_id=1, source_target_pairs={{0,12},{4,8},{8,4},{12,0},{1,13},{5,9},{9,5},{13,1},{2,14},{6,10},... | collective-permute-start | bytes 393224 | tf_op jit(solution)/shard_map/ppermute | solution.py:25
  98.6 1.3 copy-start.12
  98.7 25.8 %copy-start.6 = (bf16[32,8,8,128]{3,2,1,0:T(8,128)(2,1)}, bf16[32,8,8,128]{3,2,1,0:T(8,128)(2,1)S(1)}, u32[]{:S(2)}) copy-start(bf16[32,8,8,128]{3,2,1,0:T(8,128)(2,1)S(1)} %copy.69) | copy-start | bytes 1572868
  100.0 25.2 %copy-start.15 = (f32[256,256]{1,0:T(8,128)}, f32[256,256]{1,0:T(8,128)S(1)}, u32[]{:S(2)}) copy-start(f32[256,256]{1,0:T(8,128)S(1)} %fusion.62) | copy-start | bytes 786436
  120.7 3.8 %copy-start.8 = (f32[8,128,128]{2,1,0:T(8,128)S(1)}, f32[8,128,128]{2,1,0:T(8,128)}, u32[]{:S(2)}) copy-start(f32[8,128,128]{2,1,0:T(8,128)} %fusion.47) | copy-start | bytes 1572868
  124.5 1.7 copy-start.14
  128.7 33.1 %all-to-all-start.5 = ((bf16[4,64,1024]{2,1,0:T(8,128)(2,1)}), bf16[4,64,1024]{2,1,0:T(8,128)(2,1)}, u32[]{:S(2)}, u32[]{:S(2)}) async-start(bf16[4,64,1024]{2,1,0:T(8,128)(2,1)} %reshape.172), calls=%async_computation.5 | async-start | bytes 1048576 | tf_op jit(solution)/shard_map/all_to_all | solution.py:158
  132.8 1.8 copy-start.9
  132.8 1.8 copy-start.13
  134.6 1.0 copy-start.11
  134.6 1.1 copy-start.16
  161.8 31.4 %all-to-all-start.4 = ((bf16[4,64,1024]{2,1,0:T(8,128)(2,1)}), bf16[4,64,1024]{2,1,0:T(8,128)(2,1)}, u32[]{:S(2)}, u32[]{:S(2)}) async-start(bf16[4,64,1024]{2,1,0:T(8,128)(2,1)} %reshape.170), calls=%async_computation.4 | async-start | bytes 1048576 | tf_op jit(solution)/shard_map/all_to_all | solution.py:157
  184.9 3.8 %copy-start.5 = (bf16[256,8,128]{0,2,1:T(8,128)(2,1)S(1)}, bf16[256,8,128]{0,2,1:T(8,128)(2,1)}, u32[]{:S(2)}) copy-start(bf16[256,8,128]{0,2,1:T(8,128)(2,1)} %copy-done.4) | copy-start | bytes 1572868
  188.7 1.7 copy-start.7
  188.7 1.7 copy-start.17
  193.2 17.8 %all-to-all-start.2 = ((bf16[4,64,1024]{2,1,0:T(8,128)(2,1)}), bf16[4,64,1024]{2,1,0:T(8,128)(2,1)S(1)}, u32[]{:S(2)}, u32[]{:S(2)}) async-start(bf16[4,64,1024]{2,1,0:T(8,128)(2,1)} %reshape.166), calls=%async_computation.2 | async-start | bytes 1048576 | tf_op jit(solution)/shard_map/all_to_all | solution.py:156
Sparse Core Ops, SparseCore 0:
  54.9 62.5 all-gather.6
  119.1 65.7 all-gather.4
